TPU v7x, 32 devices: a whole 2x2x4 slice. The times are simulated.
32 devices in a mesh: groups: 2 (over x), expert: 16 (over z, y, core).
Axes of the slice: x: 2, y: 2, z: 4, core: 2. Of those that a mesh axis runs over, the one named last changes fastest.
Arguments:
- hidden_in: bfloat16 [256, 4096], P(('groups', 'expert')), parts along dimension 0, may hold values from -6 to 6
- queries: bfloat16 [256, 4096], P(('groups', 'expert')), parts along dimension 0, may hold values from -8 to 8
- decode_key_value: bfloat16 [256, 2, 256], P(('groups', 'expert')), parts along dimension 0, may hold values from -6 to 6
- local_kv: bfloat16 [1024, 2, 16, 256], P(('groups', 'expert')), parts along dimension 0, may hold values from -8 to 8
- page_table: int32 [256, 16], P(('groups', 'expert')), parts along dimension 0, may hold values from 0 to 31
- seq_blocks: int32 [256], P(('groups', 'expert')), parts along dimension 0, may hold values from 1 to 16
- prompt_kv: bfloat16 [32, 16, 2, 16, 256], P(('groups', 'expert')), parts along dimension 0, may hold values from -8 to 8
- prompt_owner: int32 [32], P('groups'), parts along dimension 0, may hold values from 0 to 15, as said below
- prompt_pages: int32 [32], P('groups'), parts along dimension 0, may hold values from 1 to 16
- norm_gain: float32 [4096], replicated, may hold values from 0.5 to 1.5
- router: bfloat16 [4096, 8], replicated, may hold values from -0.09375 to 0.09375
- w_gate: bfloat16 [16, 4096, 384], P('expert'), may hold values from -0.09375 to 0.09375
- w_up: bfloat16 [16, 4096, 384], P('expert'), may hold values from -0.09375 to 0.09375
- w_down: bfloat16 [16, 384, 4096], P('expert'), may hold values from -0.21875 to 0.21875
- route_ids: int32 [256, 8], P(('groups', 'expert')), parts along dimension 0, may hold values from 0 to 7, as said below
Outputs:
- layer_out: bfloat16 [256, 4096], P(('groups', 'expert')), parts along dimension 0
There are 2 independent parts, one for each index of `groups`. A program takes and returns all parts, laid end to end along the dimension named above; an argument that names none is the same for every part. Nothing has to cross between parts.
Inputs may be any that keep to these rules, and one draw needn't show every extreme that they name: `prompt_owner`: each device is named by at most 2 prompts, and by exactly 2 for some of the devices. `route_ids`: each row names 8 different experts; among the rows of one device no expert is named more than 8 times, a bound that some block reaches. `page_table`: indices among the pages of the sequence's own device.
All inputs are finite; a program needn't handle non-finite values.
Results may differ from a plain program's by a relative error of at most 0.0056.
Values may be sent and summed in bfloat16 or wider, within the bound.
No kernel may reach another device: no remote copies, remote signals or barrier semaphores. Data moves between devices by JAX's collectives and lax.ppermute only.
A program may use at most 128 MiB of HBM per device.

v0:
```python
import math
import jax
import jax.numpy as jnp
from jax import lax
from jax.sharding import PartitionSpec as P

D = 4096
QUERY_HEADS = 32
KEY_VALUE_HEADS = 2
HEAD_SIZE = 128
PAGE_TOKENS = 16
TOPK = 8
MAXB = 16
MAXP = 2
norm_eps = 1e-06
masked_score = -1e30


def partner(x, axis, apart):
    return lax.ppermute(x, axis, [(i, i ^ 1 << apart) for i in range(lax.axis_size(axis))])


def attend(rows_of_queries, rows_of_keys, rows_of_values, allowed, token_own_key, token_own_value):
    decode_tokens = rows_of_queries.shape[0]
    heads_of_queries = rows_of_queries.reshape(
        decode_tokens, KEY_VALUE_HEADS, QUERY_HEADS // KEY_VALUE_HEADS, HEAD_SIZE
    )
    heads_of_keys = rows_of_keys.reshape(decode_tokens, -1, KEY_VALUE_HEADS, HEAD_SIZE)
    heads_of_values = rows_of_values.reshape(decode_tokens, -1, KEY_VALUE_HEADS, HEAD_SIZE)
    scale_for_scores = 1.0 / math.sqrt(HEAD_SIZE)
    allowed_mask = allowed[:, None, None, :]
    scores = (
        jnp.einsum(
            "tkgd,tlkd->tkgl", heads_of_queries, heads_of_keys, preferred_element_type=jnp.float32
        )
        * scale_for_scores
    )
    scores = jnp.where(allowed_mask, scores, masked_score)
    token_own_score = (
        jnp.einsum(
            "xejp,xep->xej",
            heads_of_queries,
            token_own_key.reshape(decode_tokens, KEY_VALUE_HEADS, HEAD_SIZE),
            preferred_element_type=jnp.float32,
        )
        * scale_for_scores
    )
    peak = jnp.maximum(jnp.max(scores, -1), token_own_score)
    weights = jnp.where(allowed_mask, jnp.exp(scores - peak[..., None]), 0.0)
    own_weight = jnp.exp(token_own_score - peak)
    denominator = jnp.sum(weights, -1) + own_weight
    probs = (weights / denominator[..., None]).astype(jnp.bfloat16)
    token_own_probability = (own_weight / denominator).astype(jnp.bfloat16)
    blended_noise = jnp.einsum(
        "tkgl,tlkd->tkgd", probs, heads_of_values, preferred_element_type=jnp.float32
    )
    blended_noise = blended_noise + token_own_probability.astype(jnp.float32)[
        ..., None
    ] * token_own_value.reshape(decode_tokens, KEY_VALUE_HEADS, 1, HEAD_SIZE).astype(jnp.float32)
    return blended_noise.reshape(decode_tokens, QUERY_HEADS * HEAD_SIZE).astype(jnp.bfloat16)


def all_tokens(resid_wide, normed, spread, w_gate, w_up, w_down):
    devices = lax.axis_size("expert")
    seq_dev, experts = spread.shape
    expert = lax.axis_index("expert") // 2
    bits = devices.bit_length() - 1
    coarse = lax.reduce_precision(spread, 8, 7)
    fine = spread - coarse
    pad = -2 * experts % 128
    tail = jnp.pad(jnp.concatenate([coarse, fine], 1), ((0, 0), (0, pad))).astype(jnp.bfloat16)
    rows = jnp.concatenate([normed, tail], 1)
    for bit in reversed(range(bits)):
        rows = jnp.concatenate([rows, partner(rows, "expert", bit)], 0)
    gates = rows[:, D : D + 2 * experts].astype(jnp.float32).reshape(-1, 2, experts)
    own = jnp.arange(experts, dtype=jnp.int32) == expert
    gate = jnp.sum(jnp.where(own, gates, 0.0), (1, 2))
    tokens = rows[:, :D]
    gate_proj = jnp.dot(tokens, w_gate, preferred_element_type=jnp.float32)
    up_proj = jnp.dot(tokens, w_up, preferred_element_type=jnp.float32)
    activated = (jax.nn.silu(gate_proj) * up_proj).astype(jnp.bfloat16)
    mixed = jnp.dot(activated, w_down, preferred_element_type=jnp.float32) * gate[:, None]
    for bit in range(bits):
        half = mixed.shape[0] // 2
        moved = partner(mixed[half:].astype(jnp.bfloat16), "expert", bit)
        mixed = mixed[:half] + moved.astype(jnp.float32)
    return (resid_wide + mixed).astype(jnp.bfloat16)


def local(
    hidden_in,
    queries,
    decode_key_value,
    local_kv,
    page_table,
    seq_blocks,
    prompt_kv,
    prompt_owner,
    prompt_pages,
    norm_gain,
    router,
    w_gate,
    w_up,
    w_down,
    route_ids,
):
    devices = lax.axis_size("expert")
    position = lax.axis_index("expert")
    experts = devices // 2
    seq_dev = hidden_in.shape[0]
    key_value_width = KEY_VALUE_HEADS * HEAD_SIZE
    capacity = min(seq_dev, max(2, 2 * ((3 * seq_dev * TOPK + 2 * devices - 1) // (2 * devices))))
    half_cap = capacity // 2
    even_core = position % 2 == 0
    prompt_count = prompt_owner.shape[0]
    prompt_range = jnp.arange(prompt_count, dtype=jnp.int32)
    same_owner = prompt_owner[:, None] == prompt_owner[None, :]
    earlier = prompt_range[None, :] < prompt_range[:, None]
    arrival = jnp.sum((same_owner & earlier).astype(jnp.int32), 1)
    matching = (
        prompt_owner[None, None, :] == jnp.arange(devices, dtype=jnp.int32)[:, None, None]
    ) & (arrival[None, None, :] == jnp.arange(MAXP, dtype=jnp.int32)[None, :, None])
    chosen_prompt = jnp.sum(jnp.where(matching, prompt_range[None, None, :], 0), -1)
    occupied = jnp.any(matching, -1)
    own_picks = lax.dynamic_index_in_dim(chosen_prompt, position, 0, keepdims=False)
    own_occupied = lax.dynamic_index_in_dim(occupied, position, 0, keepdims=False)
    page_rows = prompt_kv[0]
    outgoing = jnp.take(page_rows, chosen_prompt.T.reshape(-1), axis=0).reshape(
        MAXP, devices, 2, PAGE_TOKENS, key_value_width
    )
    outgoing = jnp.where(occupied.T[:, :, None, None, None], outgoing, 0)
    arrived = lax.all_to_all(outgoing, "expert", split_axis=1, concat_axis=1, tiled=True)
    lengths = jnp.take(prompt_pages, own_picks)
    new_keys = arrived[:, :, 0].reshape(MAXP, devices * PAGE_TOKENS, key_value_width)
    new_values = arrived[:, :, 1].reshape(MAXP, devices * PAGE_TOKENS, key_value_width)
    new_allowed = (jnp.arange(devices * PAGE_TOKENS, dtype=jnp.int32) // PAGE_TOKENS)[
        None, :
    ] < lengths[:, None]
    fresh_rows = attend(
        queries[:MAXP],
        new_keys,
        new_values,
        new_allowed,
        decode_key_value[:MAXP, 0],
        decode_key_value[:MAXP, 1],
    )
    fetched = local_kv[page_table]
    old_keys = fetched[:, :, 0].reshape(seq_dev, MAXB * PAGE_TOKENS, key_value_width)
    old_values = fetched[:, :, 1].reshape(seq_dev, MAXB * PAGE_TOKENS, key_value_width)
    old_allowed = (jnp.arange(MAXB * PAGE_TOKENS, dtype=jnp.int32) // PAGE_TOKENS)[
        None, :
    ] < seq_blocks[:, None]
    old_out = attend(
        queries, old_keys, old_values, old_allowed, decode_key_value[:, 0], decode_key_value[:, 1]
    )
    new_count = jnp.sum(own_occupied.astype(jnp.int32))
    is_new = jnp.arange(MAXP, dtype=jnp.int32) < new_count
    attention = jnp.concatenate(
        [jnp.where(is_new[:, None], fresh_rows, old_out[:MAXP]), old_out[MAXP:]], 0
    )
    residual = (hidden_in.astype(jnp.float32) + attention.astype(jnp.float32)).astype(jnp.bfloat16)
    resid_wide = residual.astype(jnp.float32)
    normed = (
        resid_wide
        * lax.rsqrt(jnp.mean(resid_wide * resid_wide, -1, keepdims=True) + norm_eps)
        * norm_gain
    ).astype(jnp.bfloat16)
    logits = jnp.dot(normed, router, preferred_element_type=jnp.float32)
    expert_onehot = route_ids[:, :, None] == jnp.arange(experts, dtype=jnp.int32)[None, None, :]
    selected = jnp.sum(jnp.where(expert_onehot, logits[:, None, :], 0.0), -1)
    gate_weights = jax.nn.softmax(selected, -1)
    if capacity >= seq_dev and devices & devices - 1 == 0:
        spread = jnp.sum(jnp.where(expert_onehot, gate_weights[:, :, None], 0.0), 1)
        return all_tokens(resid_wide, normed, spread, w_gate[0], w_up[0], w_down[0])
    assigned = seq_dev * TOPK
    expert_ids = route_ids.reshape(assigned)
    chosen = (expert_ids[:, None] == jnp.arange(experts, dtype=jnp.int32)[None, :]).astype(
        jnp.int32
    )
    before = jnp.cumsum(chosen, 0) - chosen
    slot_rank = jnp.sum(before * chosen, 1)
    slot_index = expert_ids * capacity + slot_rank
    placing = slot_index[None, :] == jnp.arange(experts * capacity, dtype=jnp.int32)[:, None]
    selector = jnp.any(placing.reshape(experts * capacity, seq_dev, TOPK), -1).astype(jnp.bfloat16)
    gathered_rows = jnp.dot(selector, normed, preferred_element_type=jnp.float32).astype(
        jnp.bfloat16
    )
    outgoing_half = gathered_rows.reshape(devices, half_cap, D)
    own_half = lax.all_to_all(outgoing_half, "expert", split_axis=0, concat_axis=0, tiled=True)
    partner_half = partner(own_half, "expert", 0)
    received = jnp.where(
        even_core,
        jnp.concatenate([own_half, partner_half], 1),
        jnp.concatenate([partner_half, own_half], 1),
    )
    flattened = received.reshape(devices * capacity, D)
    gate_proj = jnp.dot(flattened, w_gate[0], preferred_element_type=jnp.float32)
    up_proj = jnp.dot(flattened, w_up[0], preferred_element_type=jnp.float32)
    activated = (jax.nn.silu(gate_proj) * up_proj).astype(jnp.bfloat16)
    partial_value = jnp.dot(activated, w_down[0], preferred_element_type=jnp.float32).reshape(
        devices, capacity, D
    )
    kept = jnp.where(even_core, partial_value[:, :half_cap], partial_value[:, half_cap:])
    handed = jnp.where(even_core, partial_value[:, half_cap:], partial_value[:, :half_cap])
    partner_part = partner(handed, "expert", 0)
    finished = (kept + partner_part).astype(jnp.bfloat16)
    returned = lax.all_to_all(finished, "expert", split_axis=0, concat_axis=0, tiled=True)
    expert_sum = returned.reshape(experts * capacity, D)
    picked = jnp.take(expert_sum, slot_index, axis=0).astype(jnp.float32).reshape(seq_dev, TOPK, D)
    expert_mix = jnp.sum(picked * gate_weights[:, :, None], 1)
    return (resid_wide + expert_mix).astype(jnp.bfloat16)


def solution(mesh):
    return jax.shard_map(
        local,
        mesh=mesh,
        in_specs=(
            P(("groups", "expert"), None),
            P(("groups", "expert"), None),
            P(("groups", "expert"), None, None),
            P(("groups", "expert"), None, None, None),
            P(("groups", "expert"), None),
            P(("groups", "expert")),
            P(("groups", "expert"), None, None, None, None),
            P("groups"),
            P("groups"),
            P(),
            P(),
            P("expert", None, None),
            P("expert", None, None),
            P("expert", None, None),
            P(("groups", "expert"), None),
        ),
        out_specs=P(("groups", "expert"), None),
        check_vma=False,
    )
```

profile of v0, /device:TPU:0, one launch (start us, length us, event | category | flops | bytes accessed | tf_op | source)
XLA Modules:
  0.0 98.2 jit_solution(18162269884148207099)
XLA Ops:
  2.8 2.3 %gather_fusion.1 = bf16[32,2,16,256]{3,2,1,0:T(8,128)(2,1)} fusion(bf16[16,2,16,256]{3,2,1,0:T(8,128)(2,1)} %bitcast.87, s32[1024]{0:T(1024)S(1)} %get-tuple-element.26), kind=kCustom, calls=%fused_computation.1 | custom fusion | bytes 1048704 | tf_op jit(solution)/shard_map/jit(_take)/gather | solution.py:128
  7.2 7.5 %all-to-all-start = ((bf16[2,16,2,16,256]{4,3,0,2,1:T(8,128)(2,1)}), bf16[2,16,2,16,256]{4,3,0,2,1:T(8,128)(2,1)}, u32[]{:S(2)}, u32[]{:S(2)}) async-start(bf16[2,16,2,16,256]{4,3,0,2,1:T(8,128)(2,1)} %copy.48), calls=%async_computation | async-start | bytes 1048576 | tf_op jit(solution)/shard_map/all_to_all | solution.py:132
  14.7 3.1 %gather_fusion.2 = bf16[128,2,16,256]{3,2,1,0:T(8,128)(2,1)} fusion(bf16[32,2,16,256]{3,2,1,0:T(8,128)(2,1)} %param.18, s32[1024]{0:T(1024)S(1)} %get-tuple-element.25), kind=kCustom, calls=%fused_computation.2 | custom fusion | bytes 4194816 | tf_op jit(solution)/shard_map/gather | solution.py:147
  17.8 3.0 %slice_bitcast_fusion.1 = (bf16[8,16,1,16,256]{4,3,1,0,2:T(8,128)(2,1)}, bf16[8,16,1,16,256]{4,3,1,0,2:T(8,128)(2,1)}) fusion(bf16[8,16,2,16,256]{4,3,2,1,0:T(8,128)(2,1)} %bitcast.85), kind=kLoop, calls=%fused_computation.22 | loop fusion | bytes 4194304
  20.8 2.2 %reshape_reshape_squeeze.15 = bf16[8,256,2,128]{3,2,1,0:T(2,128)(2,1)} reshape(bf16[8,16,1,16,256]{4,3,1,0,2:T(8,128)(2,1)} %get-tuple-element.8) | data formatting | bytes 2097152 | tf_op jit(solution)/shard_map/reshape;reshape;squeeze | solution.py:29
  23.0 2.2 %reshape_reshape_squeeze.14 = bf16[8,256,2,128]{3,2,1,0:T(2,128)(2,1)} reshape(bf16[8,16,1,16,256]{4,3,1,0,2:T(8,128)(2,1)} %get-tuple-element.7) | data formatting | bytes 2097152 | tf_op jit(solution)/shard_map/reshape;reshape;squeeze | solution.py:28
  25.5 1.8 %fusion.66 = (f32[8,2,16]{2,1,0:T(2,128)S(1)}, f32[8,2,16,256]{3,2,1,0:T(8,128)S(1)}) fusion(bf16[8,2,16,128]{3,0,2,1:T(8,128)(2,1)S(1)} %bitcast.103, bf16[8,256,2,128]{3,2,1,0:T(2,128)(2,1)} %reshape_reshape_squeeze.14, pred[8,256]{1,0:T(8,128)(4,1)S(1)} %broadcast_compare_fusion), kind=kOutput, calls=%fused_computation.142 | convolution fusion | flops 16973568 | bytes 1379328 | tf_op jit(solution)/shard_map/tkgd,tlkd->tkgl/dot_general | solution.py:33
  32.4 1.8 %fusion.65 = (bf16[2,16,1,16,256]{4,3,0,2,1:T(8,128)(2,1)}, bf16[2,16,1,16,256]{4,3,0,2,1:T(8,128)(2,1)S(1)}) fusion(bf16[2,16,2,16,256]{4,3,0,2,1:T(8,128)(2,1)} %all-to-all-done), kind=kLoop, calls=%fused_computation.141 | loop fusion | bytes 1048576 | tf_op jit(solution)/shard_map/slice | solution.py:134
  43.9 2.8 %collective-permute-start = (bf16[8,4224]{1,0:T(8,128)(2,1)S(1)}, bf16[8,4224]{1,0:T(8,128)(2,1)S(1)}, u32[]{:S(2)}, u32[]{:S(2)}) collective-permute-start(bf16[8,4224]{1,0:T(8,128)(2,1)S(1)} %get-tuple-element.11), channel_id=1, source_target_pairs={{0,8},{1,9},{2,10},{3,11},{4,12},{5,13},{6,14},{7,15},{8,0},{9,1},... | collective-permute-start | bytes 202760 | tf_op jit(solution)/shard_map/ppermute | solution.py:20
  46.8 3.9 %collective-permute-done = bf16[8,4224]{1,0:T(8,128)(2,1)S(1)} collective-permute-done((bf16[8,4224]{1,0:T(8,128)(2,1)S(1)}, bf16[8,4224]{1,0:T(8,128)(2,1)S(1)}, u32[]{:S(2)}, u32[]{:S(2)}) %collective-permute-start) | collective-permute-done | bytes 67616 | tf_op jit(solution)/shard_map/ppermute | solution.py:20
  52.0 3.8 %collective-permute-done.1 = bf16[16,4224]{1,0:T(8,128)(2,1)S(1)} collective-permute-done((bf16[16,4224]{1,0:T(8,128)(2,1)S(1)}, bf16[16,4224]{1,0:T(8,128)(2,1)S(1)}, u32[]{:S(2)}, u32[]{:S(2)}) %collective-permute-start.1) | collective-permute-done | bytes 135200 | tf_op jit(solution)/shard_map/ppermute | solution.py:20
  55.8 1.8 %collective-permute-start.2 = (bf16[32,4224]{1,0:T(8,128)(2,1)S(1)}, bf16[32,4224]{1,0:T(8,128)(2,1)S(1)}, u32[]{:S(2)}, u32[]{:S(2)}) collective-permute-start(bf16[32,4224]{1,0:T(8,128)(2,1)S(1)} %pad_maximum_fusion.1), channel_id=1, source_target_pairs={{0,2},{1,3},{2,0},{3,1},{4,6},{5,7},{6,4},{7,5},{8,10},{9,11},{10,... | collective-permute-start | bytes 811016 | tf_op jit(solution)/shard_map/ppermute | solution.py:20
  58.3 4.0 %collective-permute-done.2 = bf16[32,4224]{1,0:T(8,128)(2,1)S(1)} collective-permute-done((bf16[32,4224]{1,0:T(8,128)(2,1)S(1)}, bf16[32,4224]{1,0:T(8,128)(2,1)S(1)}, u32[]{:S(2)}, u32[]{:S(2)}) %collective-permute-start.2) | collective-permute-done | bytes 270368 | tf_op jit(solution)/shard_map/ppermute | solution.py:20
  66.1 1.9 %fusion.1 = f32[128,384]{1,0:T(8,128)S(1)} fusion(bf16[1,4096,384]{2,1,0:T(8,128)(2,1)S(1)} %copy-done.2, bf16[128,4224]{1,0:T(8,128)(2,1)} %constant_dynamic-update-slice_fusion), kind=kOutput, calls=%fused_computation.5 | convolution fusion | flops 402653184 | bytes 4390912 | tf_op jit(solution)/shard_map/dot_general | solution.py:80
  68.0 5.0 %convolution_multiply_fusion = f32[128,4096]{1,0:T(8,128)} fusion(bf16[1,384,4096]{2,1,0:T(8,128)(2,1)S(1)} %copy-done, f32[128]{0:T(128)S(1)} %select_reduce_fusion, f32[128,384]{1,0:T(8,128)S(1)} %fusion.1, bf16[1,4096,384]{2,1,0:T(8,128)(2,1)} %param.26, bf16[128,4224]{1,0:T(8,128)(2,1)} %constant_dynamic-update-slice_fusion), kind=kOutput, calls=%fused_computation.3 | convolution fusion | flops 806125568 | bytes 9634304 | tf_op jit(solution)/shard_map/dot_general | solution.py:82
  73.0 1.3 %slice.146 = bf16[64,4096]{1,0:T(8,128)(2,1)S(1)} slice(f32[128,4096]{1,0:T(8,128)} %convolution_multiply_fusion), slice={[64:128], [0:4096]} | slice | bytes 1048576 | tf_op jit(solution)/shard_map/slice | solution.py:85
  74.5 1.8 %collective-permute-done.4 = bf16[64,4096]{1,0:T(8,128)(2,1)S(1)} collective-permute-done((bf16[64,4096]{1,0:T(8,128)(2,1)S(1)}, bf16[64,4096]{1,0:T(8,128)(2,1)S(1)}, u32[]{:S(2)}, u32[]{:S(2)}) %collective-permute-start.4) | collective-permute-done | bytes 524320 | tf_op jit(solution)/shard_map/ppermute | solution.py:20
  76.3 1.3 %slice_add_fusion = f32[64,4096]{1,0:T(8,128)S(1)} fusion(f32[128,4096]{1,0:T(8,128)} %convolution_multiply_fusion, bf16[64,4096]{1,0:T(8,128)(2,1)S(1)} %collective-permute-done.4), kind=kLoop, calls=%fused_computation.20 | loop fusion | flops 524288 | bytes 2621440 | tf_op jit(solution)/shard_map/add | solution.py:86
  77.6 1.8 %collective-permute-start.5 = (bf16[32,4096]{1,0:T(8,128)(2,1)S(1)}, bf16[32,4096]{1,0:T(8,128)(2,1)S(1)}, u32[]{:S(2)}, u32[]{:S(2)}) collective-permute-start(bf16[32,4096]{1,0:T(8,128)(2,1)S(1)} %slice.147), channel_id=1, source_target_pairs={{0,2},{1,3},{2,0},{3,1},{4,6},{5,7},{6,4},{7,5},{8,10},{9,11},{10,... | collective-permute-start | bytes 786440 | tf_op jit(solution)/shard_map/ppermute | solution.py:20
  79.4 6.6 %collective-permute-done.5 = bf16[32,4096]{1,0:T(8,128)(2,1)S(1)} collective-permute-done((bf16[32,4096]{1,0:T(8,128)(2,1)S(1)}, bf16[32,4096]{1,0:T(8,128)(2,1)S(1)}, u32[]{:S(2)}, u32[]{:S(2)}) %collective-permute-start.5) | collective-permute-done | bytes 262176 | tf_op jit(solution)/shard_map/ppermute | solution.py:20
  86.1 2.2 %collective-permute-start.6 = (bf16[16,4096]{1,0:T(8,128)(2,1)S(1)}, bf16[16,4096]{1,0:T(8,128)(2,1)S(1)}, u32[]{:S(2)}, u32[]{:S(2)}) collective-permute-start(bf16[16,4096]{1,0:T(8,128)(2,1)S(1)} %slice.148), channel_id=1, source_target_pairs={{0,4},{1,5},{2,6},{3,7},{4,0},{5,1},{6,2},{7,3},{8,12},{9,13},{10,... | collective-permute-start | bytes 393224 | tf_op jit(solution)/shard_map/ppermute | solution.py:20
  88.3 2.9 %collective-permute-done.6 = bf16[16,4096]{1,0:T(8,128)(2,1)S(1)} collective-permute-done((bf16[16,4096]{1,0:T(8,128)(2,1)S(1)}, bf16[16,4096]{1,0:T(8,128)(2,1)S(1)}, u32[]{:S(2)}, u32[]{:S(2)}) %collective-permute-start.6) | collective-permute-done | bytes 131104 | tf_op jit(solution)/shard_map/ppermute | solution.py:20
  91.3 4.0 %collective-permute-start.7 = (bf16[8,4096]{1,0:T(8,128)(2,1)S(1)}, bf16[8,4096]{1,0:T(8,128)(2,1)S(1)}, u32[]{:S(2)}, u32[]{:S(2)}) collective-permute-start(bf16[8,4096]{1,0:T(8,128)(2,1)S(1)} %slice.149), channel_id=1, source_target_pairs={{0,8},{1,9},{2,10},{3,11},{4,12},{5,13},{6,14},{7,15},{8,0},{9,1},... | collective-permute-start | bytes 196616 | tf_op jit(solution)/shard_map/ppermute | solution.py:20
  95.3 2.2 %collective-permute-done.7 = bf16[8,4096]{1,0:T(8,128)(2,1)S(1)} collective-permute-done((bf16[8,4096]{1,0:T(8,128)(2,1)S(1)}, bf16[8,4096]{1,0:T(8,128)(2,1)S(1)}, u32[]{:S(2)}, u32[]{:S(2)}) %collective-permute-start.7) | collective-permute-done | bytes 65568 | tf_op jit(solution)/shard_map/ppermute | solution.py:20
  (109 shorter events, 26.7 us)
Async XLA Ops:
  0.0 68.0 %copy-start = (bf16[1,384,4096]{2,1,0:T(8,128)(2,1)S(1)}, bf16[1,384,4096]{2,1,0:T(8,128)(2,1)}, u32[]{:S(2)}) copy-start(bf16[1,384,4096]{2,1,0:T(8,128)(2,1)} %param.28) | copy-start | bytes 9437188
  7.2 25.2 %all-to-all-start = ((bf16[2,16,2,16,256]{4,3,0,2,1:T(8,128)(2,1)}), bf16[2,16,2,16,256]{4,3,0,2,1:T(8,128)(2,1)}, u32[]{:S(2)}, u32[]{:S(2)}) async-start(bf16[2,16,2,16,256]{4,3,0,2,1:T(8,128)(2,1)} %copy.48), calls=%async_computation | async-start | bytes 1048576 | tf_op jit(solution)/shard_map/all_to_all | solution.py:132
  23.0 2.2 %copy-start.7 = (bf16[8,2,256]{2,1,0:T(2,128)(2,1)S(1)}, bf16[8,2,256]{2,1,0:T(2,128)(2,1)}, u32[]{:S(2)}) copy-start(bf16[8,2,256]{2,1,0:T(2,128)(2,1)} %param.17) | copy-start | bytes 24580
  23.0 2.3 %copy-start.13 = (s32[8]{0:T(128)S(1)}, s32[8]{0:T(128)}, u32[]{:S(2)}) copy-start(s32[8]{0:T(128)} %param.20) | copy-start | bytes 100
  23.0 2.4 %copy-start.11 = (bf16[8,4096]{1,0:T(8,128)(2,1)S(1)}, bf16[8,4096]{1,0:T(8,128)(2,1)}, u32[]{:S(2)}) copy-start(bf16[8,4096]{1,0:T(8,128)(2,1)} %param.16) | copy-start | bytes 196612
  25.5 2.1 %copy-start.3 = (bf16[8,256,2,128]{3,2,1,0:T(2,128)(2,1)S(1)}, bf16[8,256,2,128]{3,2,1,0:T(2,128)(2,1)}, u32[]{:S(2)}) copy-start(bf16[8,256,2,128]{3,2,1,0:T(2,128)(2,1)} %reshape_reshape_squeeze.15) | copy-start | bytes 3145732
  27.5 1.2 %copy-start.1 = (s32[16]{0:T(128)S(1)}, s32[16]{0:T(128)}, u32[]{:S(2)}) copy-start(s32[16]{0:T(128)} %param.23) | copy-start | bytes 196
  27.9 6.3 %copy-start.4 = (bf16[8,2,16,128]{3,2,1,0:T(8,128)(2,1)}, bf16[8,2,16,128]{3,2,1,0:T(8,128)(2,1)S(1)}, u32[]{:S(2)}) copy-start(bf16[8,2,16,128]{3,2,1,0:T(8,128)(2,1)S(1)} %fusion.7) | copy-start | bytes 196612
  28.7 5.4 %copy-start.10 = (bf16[1,2,32,128]{3,2,1,0:T(8,128)(2,1)}, bf16[1,2,32,128]{3,2,1,0:T(8,128)(2,1)S(1)}, u32[]{:S(2)}) copy-start(bf16[1,2,32,128]{3,2,1,0:T(8,128)(2,1)S(1)} %copy.66) | copy-start | bytes 49156
  34.9 6.4 %slice-start = ((bf16[8,2,16,128]{3,2,1,0:T(8,128)(2,1)}), bf16[2,2,16,128]{3,2,1,0:T(8,128)(2,1)S(1)}, s32[]{:S(2)}) async-start(bf16[8,2,16,128]{3,2,1,0:T(8,128)(2,1)} %copy-done.4), calls=%async_computation.1 | async-start | bytes 32768 | tf_op jit(solution)/shard_map/slice | solution.py:159
  34.9 6.5 %copy-start.5 = (bf16[8,4096]{1,0:T(8,128)(2,1)S(1)}, bf16[8,4096]{1,0:T(8,128)(2,1)}, u32[]{:S(2)}) copy-start(bf16[8,4096]{1,0:T(8,128)(2,1)} %param.15) | copy-start | bytes 196612
  36.7 4.6 %copy-start.12 = (pred[2]{0:T(512)(128)(4,1)S(1)}, pred[2]{0:T(512)(128)(4,1)}, u32[]{:S(2)}) copy-start(pred[2]{0:T(512)(128)(4,1)} %iota_compare_fusion.6) | copy-start | bytes 10
  36.7 4.9 %copy-start.8 = (f32[4096]{0:T(1024)S(1)}, f32[4096]{0:T(1024)}, u32[]{:S(2)}) copy-start(f32[4096]{0:T(1024)} %param.24) | copy-start | bytes 49156
  36.7 5.0 %copy-start.6 = (bf16[4096,8]{0,1:T(8,128)(2,1)S(1)}, bf16[4096,8]{0,1:T(8,128)(2,1)}, u32[]{:S(2)}) copy-start(bf16[4096,8]{0,1:T(8,128)(2,1)} %param.25) | copy-start | bytes 196612
  36.7 5.2 %copy-start.9 = (s32[8,8]{1,0:T(8,128)S(1)}, s32[8,8]{1,0:T(8,128)}, u32[]{:S(2)}) copy-start(s32[8,8]{1,0:T(8,128)} %param.29) | copy-start | bytes 772
  43.9 6.7 %collective-permute-start = (bf16[8,4224]{1,0:T(8,128)(2,1)S(1)}, bf16[8,4224]{1,0:T(8,128)(2,1)S(1)}, u32[]{:S(2)}, u32[]{:S(2)}) collective-permute-start(bf16[8,4224]{1,0:T(8,128)(2,1)S(1)} %get-tuple-element.11), channel_id=1, source_target_pairs={{0,8},{1,9},{2,10},{3,11},{4,12},{5,13},{6,14},{7,15},{8,0},{9,1},... | collective-permute-start | bytes 202760 | tf_op jit(solution)/shard_map/ppermute | solution.py:20
  50.7 5.1 %collective-permute-start.1 = (bf16[16,4224]{1,0:T(8,128)(2,1)S(1)}, bf16[16,4224]{1,0:T(8,128)(2,1)S(1)}, u32[]{:S(2)}, u32[]{:S(2)}) collective-permute-start(bf16[16,4224]{1,0:T(8,128)(2,1)S(1)} %pad_maximum_fusion.2), channel_id=1, source_target_pairs={{0,4},{1,5},{2,6},{3,7},{4,0},{5,1},{6,2},{7,3},{8,12},{9,13},{10,... | collective-permute-start | bytes 405512 | tf_op jit(solution)/shard_map/ppermute | solution.py:20
  55.8 10.3 %copy-start.2 = (bf16[1,4096,384]{2,1,0:T(8,128)(2,1)S(1)}, bf16[1,4096,384]{2,1,0:T(8,128)(2,1)}, u32[]{:S(2)}) copy-start(bf16[1,4096,384]{2,1,0:T(8,128)(2,1)} %param.27) | copy-start | bytes 9437188
  55.8 6.5 %collective-permute-start.2 = (bf16[32,4224]{1,0:T(8,128)(2,1)S(1)}, bf16[32,4224]{1,0:T(8,128)(2,1)S(1)}, u32[]{:S(2)}, u32[]{:S(2)}) collective-permute-start(bf16[32,4224]{1,0:T(8,128)(2,1)S(1)} %pad_maximum_fusion.1), channel_id=1, source_target_pairs={{0,2},{1,3},{2,0},{3,1},{4,6},{5,7},{6,4},{7,5},{8,10},{9,11},{10,... | collective-permute-start | bytes 811016 | tf_op jit(solution)/shard_map/ppermute | solution.py:20
  62.4 2.0 %collective-permute-start.3 = (bf16[64,4224]{1,0:T(8,128)(2,1)S(1)}, bf16[64,4224]{1,0:T(8,128)(2,1)S(1)}, u32[]{:S(2)}, u32[]{:S(2)}) collective-permute-start(bf16[64,4224]{1,0:T(8,128)(2,1)S(1)} %pad_maximum_fusion), channel_id=1, source_target_pairs={{0,1},{1,0},{2,3},{3,2},{4,5},{5,4},{6,7},{7,6},{8,9},{9,8},{10,11... | collective-permute-start | bytes 1622024 | tf_op jit(solution)/shard_map/ppermute | solution.py:20
  74.3 2.0 %collective-permute-start.4 = (bf16[64,4096]{1,0:T(8,128)(2,1)S(1)}, bf16[64,4096]{1,0:T(8,128)(2,1)S(1)}, u32[]{:S(2)}, u32[]{:S(2)}) collective-permute-start(bf16[64,4096]{1,0:T(8,128)(2,1)S(1)} %slice.146), channel_id=1, source_target_pairs={{0,1},{1,0},{2,3},{3,2},{4,5},{5,4},{6,7},{7,6},{8,9},{9,8},{10,11... | collective-permute-start | bytes 1572872 | tf_op jit(solution)/shard_map/ppermute | solution.py:20
  77.6 8.4 %collective-permute-start.5 = (bf16[32,4096]{1,0:T(8,128)(2,1)S(1)}, bf16[32,4096]{1,0:T(8,128)(2,1)S(1)}, u32[]{:S(2)}, u32[]{:S(2)}) collective-permute-start(bf16[32,4096]{1,0:T(8,128)(2,1)S(1)} %slice.147), channel_id=1, source_target_pairs={{0,2},{1,3},{2,0},{3,1},{4,6},{5,7},{6,4},{7,5},{8,10},{9,11},{10,... | collective-permute-start | bytes 786440 | tf_op jit(solution)/shard_map/ppermute | solution.py:20
  86.1 5.1 %collective-permute-start.6 = (bf16[16,4096]{1,0:T(8,128)(2,1)S(1)}, bf16[16,4096]{1,0:T(8,128)(2,1)S(1)}, u32[]{:S(2)}, u32[]{:S(2)}) collective-permute-start(bf16[16,4096]{1,0:T(8,128)(2,1)S(1)} %slice.148), channel_id=1, source_target_pairs={{0,4},{1,5},{2,6},{3,7},{4,0},{5,1},{6,2},{7,3},{8,12},{9,13},{10,... | collective-permute-start | bytes 393224 | tf_op jit(solution)/shard_map/ppermute | solution.py:20
  91.3 6.2 %collective-permute-start.7 = (bf16[8,4096]{1,0:T(8,128)(2,1)S(1)}, bf16[8,4096]{1,0:T(8,128)(2,1)S(1)}, u32[]{:S(2)}, u32[]{:S(2)}) collective-permute-start(bf16[8,4096]{1,0:T(8,128)(2,1)S(1)} %slice.149), channel_id=1, source_target_pairs={{0,8},{1,9},{2,10},{3,11},{4,12},{5,13},{6,14},{7,15},{8,0},{9,1},... | collective-permute-start | bytes 196616 | tf_op jit(solution)/shard_map/ppermute | solution.py:20
where the time goes:
time: 99.1 us; the launch traced here: 98.2 us
  waiting for transfers between devices  26.4 us (27%)
  local copies, waits for them, and re-layouts  23.2 us (23%)
  starting transfers between devices  21 us (21%)
  other arithmetic  14.7 us (15%)
  matrix products  12.4 us (13%)
    ppermute x8, waiting for transfers between devices, partner(): lax.ppermute(x, axis, [(i, i ^ 1 << apart) for i in range(lax.axis_size(a...  26.4 us
    ppermute x8, starting transfers between devices, partner(): lax.ppermute(x, axis, [(i, i ^ 1 << apart) for i in range(lax.axis_size(a...  13.6 us
    all_to_all x1, starting transfers between devices, local(): lax.all_to_all(outgoing, 'expert', split_axis=1, concat_axis=1, tiled=True)  7.46 us
    unnamed x36, local copies, waits for them, and re-layouts  5.18 us
    dot_general x1, matrix products, all_tokens(): jnp.dot(activated, w_down, preferred_element_type=jnp.float32)  4.98 us
    gather x1, local copies, waits for them, and re-layouts, local(): fetched = local_kv[page_table]  3.07 us
    dot_general x2, matrix products, attend(): jnp.einsum('tkgd,tlkd->tkgl', heads_of_queries, heads_of_keys, preferred_...  3.04 us
    another operation x2, local copies, waits for them, and re-layouts, attend(): rows_of_keys.reshape(decode_tokens, -1, KEY_VALUE_HEADS, HEAD_SIZE)  3 us
  transfers between devices with their start and end apart: 9, of which 8 were waited for; matrix products, arithmetic and copies ran while one was open for 20% of the time, Pallas kernels for 0%

commit v1 on v0

--- a/solution.py
+++ b/solution.py
@@ -129,7 +129,19 @@
         MAXP, devices, 2, PAGE_TOKENS, key_value_width
     )
     outgoing = jnp.where(occupied.T[:, :, None, None, None], outgoing, 0)
-    arrived = lax.all_to_all(outgoing, "expert", split_axis=1, concat_axis=1, tiled=True)
+    y2, arr_next = (lax.axis_size("expert"), lax.axis_index("expert"))
+    later = outgoing.shape[1] // y2
+    z_new = jnp.roll(outgoing, -arr_next * later, axis=1)
+    views = [lax.slice_in_dim(z_new, 0, later, axis=1)]
+    dev = 1
+    while dev < y2:
+        p_next = lax.slice_in_dim(z_new, dev * later, (dev + 1) * later, axis=1)
+        views.append(
+            lax.ppermute(p_next, axis_name="expert", perm=[(b, (b + dev) % y2) for b in range(y2)])
+        )
+        dev = dev + 1
+    shaped = jnp.concatenate(views[::-1], axis=1)
+    arrived = jnp.roll(shaped, (arr_next + 1) * views[0].shape[1], axis=1)
     lengths = jnp.take(prompt_pages, own_picks)
     new_keys = arrived[:, :, 0].reshape(MAXP, devices * PAGE_TOKENS, key_value_width)
     new_values = arrived[:, :, 1].reshape(MAXP, devices * PAGE_TOKENS, key_value_width)

time: 99.1 us -> 124 us (1.25)
  waiting for transfers between devices: 26.4 us -> 40.4 us
  starting transfers between devices: 21 us -> 25.4 us
  local copies, waits for them, and re-layouts: 23.2 us -> 27.5 us
    ppermute x0 -> x15, starting transfers between devices: none -> 21.8 us  [local(): lax.ppermute(p_next, axis_name='expert', perm=[(b, (b + dev) % y2) for b...]
    ppermute x8, starting transfers between devices: 13.6 us -> 3.64 us  [partner(): lax.ppermute(x, axis, [(i, i ^ 1 << apart) for i in range(lax.axis_size(a...]
    all_to_all x1 -> x0, starting transfers between devices: 7.46 us -> none  [local(): lax.all_to_all(outgoing, 'expert', split_axis=1, concat_axis=1, tiled=True)]
    ppermute x8, waiting for transfers between devices: 26.4 us -> 33.8 us  [partner(): lax.ppermute(x, axis, [(i, i ^ 1 << apart) for i in range(lax.axis_size(a...]
    ppermute x0 -> x15, waiting for transfers between devices: none -> 6.59 us  [local(): lax.ppermute(p_next, axis_name='expert', perm=[(b, (b + dev) % y2) for b...]
    unnamed x36 -> x51, local copies, waits for them, and re-layouts: 5.18 us -> 9.82 us
    slice x2 -> x1, local copies, waits for them, and re-layouts: 2.77 us -> 0.74 us  [local(): arrived[:, :, 0].reshape(MAXP, devices * PAGE_TOKENS, key_value_width)]
  transfers between devices with their start and end apart: 9 -> 23, of which waited for: 8 -> 12; matrix products, arithmetic and copies ran while one was open for 20% -> 20% of each run, Pallas kernels for 0% -> 0%
where the time goes in v1:
time: 124 us; the launch traced here: 123 us
  waiting for transfers between devices  40.4 us (33%)
  local copies, waits for them, and re-layouts  27.5 us (22%)
  starting transfers between devices  25.4 us (20%)
  other arithmetic  15.3 us (12%)
  matrix products  13.6 us (11%)
    ppermute x8, waiting for transfers between devices, partner(): lax.ppermute(x, axis, [(i, i ^ 1 << apart) for i in range(lax.axis_size(a...  33.8 us
    ppermute x15, starting transfers between devices, local(): lax.ppermute(p_next, axis_name='expert', perm=[(b, (b + dev) % y2) for b...  21.8 us
    unnamed x51, local copies, waits for them, and re-layouts  9.82 us
    ppermute x15, waiting for transfers between devices, local(): lax.ppermute(p_next, axis_name='expert', perm=[(b, (b + dev) % y2) for b...  6.59 us
    dot_general x1, matrix products, all_tokens(): jnp.dot(activated, w_down, preferred_element_type=jnp.float32)  4.98 us
    another operation x2, local copies, waits for them, and re-layouts, attend(): rows_of_values.reshape(decode_tokens, -1, KEY_VALUE_HEADS, HEAD_SIZE)  3.88 us
    ppermute x8, starting transfers between devices, partner(): lax.ppermute(x, axis, [(i, i ^ 1 << apart) for i in range(lax.axis_size(a...  3.64 us
    gather x1, local copies, waits for them, and re-layouts, local(): fetched = local_kv[page_table]  3.07 us
  transfers between devices with their start and end apart: 23, of which 12 were waited for; matrix products, arithmetic and copies ran while one was open for 20% of the time, Pallas kernels for 0%

profile of v1, /device:TPU:0, one launch (start us, length us, event | category | flops | bytes accessed | tf_op | source)
XLA Modules:
  0.0 122.6 jit_solution(13526682850600488801)
XLA Ops:
  2.8 2.3 %gather_fusion.1 = bf16[32,2,16,256]{3,2,1,0:T(8,128)(2,1)} fusion(bf16[16,2,16,256]{3,2,1,0:T(8,128)(2,1)} %bitcast.87, s32[1024]{0:T(1024)S(1)} %get-tuple-element.44), kind=kCustom, calls=%fused_computation.1 | custom fusion | bytes 1048704 | tf_op jit(solution)/shard_map/jit(_take)/gather | solution.py:128
  8.2 5.5 %collective-permute-start = (bf16[2,1,2,16,256]{4,3,1,0,2:T(8,128)(2,1)}, bf16[2,1,2,16,256]{4,3,1,0,2:T(8,128)(2,1)}, u32[]{:S(2)}, u32[]{:S(2)}) collective-permute-start(bf16[2,1,2,16,256]{4,3,1,0,2:T(8,128)(2,1)} %get-tuple-element.26), channel_id=1, source_target_pairs={{0,15},{1,0},{2,1},{3,2},{4,3},{5,4},{6,5},{7,6},{8,7},{9,8},{10,9... | collective-permute-start | bytes 98312 | tf_op jit(solution)/shard_map/ppermute | solution.py:140
  15.7 3.1 %gather_fusion.2 = bf16[128,2,16,256]{3,2,1,0:T(8,128)(2,1)} fusion(bf16[32,2,16,256]{3,2,1,0:T(8,128)(2,1)} %param.20, s32[1024]{0:T(1024)S(1)} %get-tuple-element.43), kind=kCustom, calls=%fused_computation.2 | custom fusion | bytes 4194816 | tf_op jit(solution)/shard_map/gather | solution.py:159
  18.8 3.1 %slice_bitcast_fusion.1 = (bf16[8,16,1,16,256]{4,3,1,0,2:T(8,128)(2,1)}, bf16[8,16,1,16,256]{4,3,1,0,2:T(8,128)(2,1)}) fusion(bf16[8,16,2,16,256]{4,3,2,1,0:T(8,128)(2,1)} %bitcast.85), kind=kLoop, calls=%fused_computation.22 | loop fusion | bytes 4194304
  21.9 2.1 %reshape_reshape_squeeze.15 = bf16[8,256,2,128]{3,2,1,0:T(2,128)(2,1)} reshape(bf16[8,16,1,16,256]{4,3,1,0,2:T(8,128)(2,1)} %get-tuple-element.9) | data formatting | bytes 2097152 | tf_op jit(solution)/shard_map/reshape;reshape;squeeze | solution.py:29
  24.0 2.2 %reshape_reshape_squeeze.14 = bf16[8,256,2,128]{3,2,1,0:T(2,128)(2,1)} reshape(bf16[8,16,1,16,256]{4,3,1,0,2:T(8,128)(2,1)} %get-tuple-element.8) | data formatting | bytes 2097152 | tf_op jit(solution)/shard_map/reshape;reshape;squeeze | solution.py:28
  26.5 1.7 %fusion.71 = (f32[8,2,16]{2,1,0:T(2,128)S(1)}, f32[8,2,16,256]{3,2,1,0:T(8,128)S(1)}) fusion(bf16[8,2,16,128]{3,0,2,1:T(8,128)(2,1)S(1)} %bitcast.103, bf16[8,256,2,128]{3,2,1,0:T(2,128)(2,1)} %reshape_reshape_squeeze.14, pred[8,256]{1,0:T(8,128)(4,1)S(1)} %broadcast_compare_fusion), kind=kOutput, calls=%fused_computation.167 | convolution fusion | flops 16973568 | bytes 1379328 | tf_op jit(solution)/shard_map/tkgd,tlkd->tkgl/dot_general | solution.py:33
  34.0 4.4 %collective-permute-start.5 = (bf16[2,1,2,16,256]{4,3,1,0,2:T(8,128)(2,1)}, bf16[2,1,2,16,256]{4,3,1,0,2:T(8,128)(2,1)S(1)}, u32[]{:S(2)}, u32[]{:S(2)}) collective-permute-start(bf16[2,1,2,16,256]{4,3,1,0,2:T(8,128)(2,1)} %get-tuple-element.21), channel_id=1, source_target_pairs={{0,10},{1,11},{2,12},{3,13},{4,14},{5,15},{6,0},{7,1},{8,2},{9,3},... | collective-permute-start | bytes 98312 | tf_op jit(solution)/shard_map/ppermute | solution.py:140
  44.2 2.7 %collective-permute-start.9 = (bf16[2,1,2,16,256]{4,3,1,0,2:T(8,128)(2,1)}, bf16[2,1,2,16,256]{4,3,1,0,2:T(8,128)(2,1)S(1)}, u32[]{:S(2)}, u32[]{:S(2)}) collective-permute-start(bf16[2,1,2,16,256]{4,3,1,0,2:T(8,128)(2,1)} %get-tuple-element.17), channel_id=1, source_target_pairs={{0,6},{1,7},{2,8},{3,9},{4,10},{5,11},{6,12},{7,13},{8,14},{9,15},... | collective-permute-start | bytes 98312 | tf_op jit(solution)/shard_map/ppermute | solution.py:140
  48.0 2.1 %collective-permute-start.11 = (bf16[2,1,2,16,256]{4,3,1,0,2:T(8,128)(2,1)}, bf16[2,1,2,16,256]{4,3,1,0,2:T(8,128)(2,1)S(1)}, u32[]{:S(2)}, u32[]{:S(2)}) collective-permute-start(bf16[2,1,2,16,256]{4,3,1,0,2:T(8,128)(2,1)} %get-tuple-element.15), channel_id=1, source_target_pairs={{0,4},{1,5},{2,6},{3,7},{4,8},{5,9},{6,10},{7,11},{8,12},{9,13},{1... | collective-permute-start | bytes 98312 | tf_op jit(solution)/shard_map/ppermute | solution.py:140
  50.1 2.0 %collective-permute-start.12 = (bf16[2,1,2,16,256]{4,3,1,0,2:T(8,128)(2,1)}, bf16[2,1,2,16,256]{4,3,1,0,2:T(8,128)(2,1)S(1)}, u32[]{:S(2)}, u32[]{:S(2)}) collective-permute-start(bf16[2,1,2,16,256]{4,3,1,0,2:T(8,128)(2,1)} %get-tuple-element.14), channel_id=1, source_target_pairs={{0,3},{1,4},{2,5},{3,6},{4,7},{5,8},{6,9},{7,10},{8,11},{9,12},{10... | collective-permute-start | bytes 98312 | tf_op jit(solution)/shard_map/ppermute | solution.py:140
  54.1 2.2 %collective-permute-done.12 = bf16[2,1,2,16,256]{4,3,1,0,2:T(8,128)(2,1)S(1)} collective-permute-done((bf16[2,1,2,16,256]{4,3,1,0,2:T(8,128)(2,1)}, bf16[2,1,2,16,256]{4,3,1,0,2:T(8,128)(2,1)S(1)}, u32[]{:S(2)}, u32[]{:S(2)}) %collective-permute-start.12) | collective-permute-done | bytes 32800 | tf_op jit(solution)/shard_map/ppermute | solution.py:140
  56.3 3.0 %collective-permute-done.13 = bf16[2,1,2,16,256]{4,3,1,0,2:T(8,128)(2,1)S(1)} collective-permute-done((bf16[2,1,2,16,256]{4,3,1,0,2:T(8,128)(2,1)}, bf16[2,1,2,16,256]{4,3,1,0,2:T(8,128)(2,1)S(1)}, u32[]{:S(2)}, u32[]{:S(2)}) %collective-permute-start.13) | collective-permute-done | bytes 32800 | tf_op jit(solution)/shard_map/ppermute | solution.py:140
  61.1 1.7 %reshape_reshape_squeeze.13 = bf16[2,256,2,128]{3,2,1,0:T(2,128)(2,1)} reshape(bf16[2,16,1,16,256]{4,3,1,0,2:T(8,128)(2,1)} %get-tuple-element.11) | data formatting | bytes 524288 | tf_op jit(solution)/shard_map/reshape;reshape;squeeze | solution.py:29
  72.2 3.8 %collective-permute-done.15 = bf16[8,4224]{1,0:T(8,128)(2,1)S(1)} collective-permute-done((bf16[8,4224]{1,0:T(8,128)(2,1)S(1)}, bf16[8,4224]{1,0:T(8,128)(2,1)S(1)}, u32[]{:S(2)}, u32[]{:S(2)}) %collective-permute-start.15) | collective-permute-done | bytes 67616 | tf_op jit(solution)/shard_map/ppermute | solution.py:20
  76.7 4.4 %collective-permute-done.16 = bf16[16,4224]{1,0:T(8,128)(2,1)S(1)} collective-permute-done((bf16[16,4224]{1,0:T(8,128)(2,1)S(1)}, bf16[16,4224]{1,0:T(8,128)(2,1)S(1)}, u32[]{:S(2)}, u32[]{:S(2)}) %collective-permute-start.16) | collective-permute-done | bytes 135200 | tf_op jit(solution)/shard_map/ppermute | solution.py:20
  81.9 5.8 %collective-permute-done.17 = bf16[32,4224]{1,0:T(8,128)(2,1)S(1)} collective-permute-done((bf16[32,4224]{1,0:T(8,128)(2,1)S(1)}, bf16[32,4224]{1,0:T(8,128)(2,1)S(1)}, u32[]{:S(2)}, u32[]{:S(2)}) %collective-permute-start.17) | collective-permute-done | bytes 270368 | tf_op jit(solution)/shard_map/ppermute | solution.py:20
  91.4 1.9 %fusion.1 = f32[128,384]{1,0:T(8,128)S(1)} fusion(bf16[1,4096,384]{2,1,0:T(8,128)(2,1)S(1)} %copy-done.2, bf16[128,4224]{1,0:T(8,128)(2,1)} %constant_dynamic-update-slice_fusion.16), kind=kOutput, calls=%fused_computation.5 | convolution fusion | flops 402653184 | bytes 4390912 | tf_op jit(solution)/shard_map/dot_general | solution.py:80
  93.4 5.0 %convolution_multiply_fusion = f32[128,4096]{1,0:T(8,128)} fusion(bf16[1,384,4096]{2,1,0:T(8,128)(2,1)S(1)} %copy-done, f32[128]{0:T(128)S(1)} %select_reduce_fusion, f32[128,384]{1,0:T(8,128)S(1)} %fusion.1, bf16[1,4096,384]{2,1,0:T(8,128)(2,1)} %param.28, bf16[128,4224]{1,0:T(8,128)(2,1)} %constant_dynamic-update-slice_fusion.16), kind=kOutput, calls=%fused_computation.3 | convolution fusion | flops 806125568 | bytes 9634304 | tf_op jit(solution)/shard_map/dot_general | solution.py:82
  99.8 1.8 %collective-permute-done.19 = bf16[64,4096]{1,0:T(8,128)(2,1)S(1)} collective-permute-done((bf16[64,4096]{1,0:T(8,128)(2,1)S(1)}, bf16[64,4096]{1,0:T(8,128)(2,1)S(1)}, u32[]{:S(2)}, u32[]{:S(2)}) %collective-permute-start.19) | collective-permute-done | bytes 524320 | tf_op jit(solution)/shard_map/ppermute | solution.py:20
  103.0 8.3 %collective-permute-done.20 = bf16[32,4096]{1,0:T(8,128)(2,1)S(1)} collective-permute-done((bf16[32,4096]{1,0:T(8,128)(2,1)S(1)}, bf16[32,4096]{1,0:T(8,128)(2,1)S(1)}, u32[]{:S(2)}, u32[]{:S(2)}) %collective-permute-start.20) | collective-permute-done | bytes 262176 | tf_op jit(solution)/shard_map/ppermute | solution.py:20
  111.5 5.0 %collective-permute-done.21 = bf16[16,4096]{1,0:T(8,128)(2,1)S(1)} collective-permute-done((bf16[16,4096]{1,0:T(8,128)(2,1)S(1)}, bf16[16,4096]{1,0:T(8,128)(2,1)S(1)}, u32[]{:S(2)}, u32[]{:S(2)}) %collective-permute-start.21) | collective-permute-done | bytes 131104 | tf_op jit(solution)/shard_map/ppermute | solution.py:20
  116.5 1.8 %collective-permute-start.22 = (bf16[8,4096]{1,0:T(8,128)(2,1)S(1)}, bf16[8,4096]{1,0:T(8,128)(2,1)S(1)}, u32[]{:S(2)}, u32[]{:S(2)}) collective-permute-start(bf16[8,4096]{1,0:T(8,128)(2,1)S(1)} %slice.230), channel_id=1, source_target_pairs={{0,8},{1,9},{2,10},{3,11},{4,12},{5,13},{6,14},{7,15},{8,0},{9,1},... | collective-permute-start | bytes 196616 | tf_op jit(solution)/shard_map/ppermute | solution.py:20
  118.3 3.6 %collective-permute-done.22 = bf16[8,4096]{1,0:T(8,128)(2,1)S(1)} collective-permute-done((bf16[8,4096]{1,0:T(8,128)(2,1)S(1)}, bf16[8,4096]{1,0:T(8,128)(2,1)S(1)}, u32[]{:S(2)}, u32[]{:S(2)}) %collective-permute-start.22) | collective-permute-done | bytes 65568 | tf_op jit(solution)/shard_map/ppermute | solution.py:20
  (153 shorter events, 42.7 us)
Async XLA Ops:
  0.0 93.4 %copy-start = (bf16[1,384,4096]{2,1,0:T(8,128)(2,1)S(1)}, bf16[1,384,4096]{2,1,0:T(8,128)(2,1)}, u32[]{:S(2)}) copy-start(bf16[1,384,4096]{2,1,0:T(8,128)(2,1)} %param.30) | copy-start | bytes 9437188
  8.2 25.8 %collective-permute-start = (bf16[2,1,2,16,256]{4,3,1,0,2:T(8,128)(2,1)}, bf16[2,1,2,16,256]{4,3,1,0,2:T(8,128)(2,1)}, u32[]{:S(2)}, u32[]{:S(2)}) collective-permute-start(bf16[2,1,2,16,256]{4,3,1,0,2:T(8,128)(2,1)} %get-tuple-element.26), channel_id=1, source_target_pairs={{0,15},{1,0},{2,1},{3,2},{4,3},{5,4},{6,5},{7,6},{8,7},{9,8},{10,9... | collective-permute-start | bytes 98312 | tf_op jit(solution)/shard_map/ppermute | solution.py:140
  13.7 25.5 %collective-permute-start.1 = (bf16[2,1,2,16,256]{4,3,1,0,2:T(8,128)(2,1)}, bf16[2,1,2,16,256]{4,3,1,0,2:T(8,128)(2,1)}, u32[]{:S(2)}, u32[]{:S(2)}) collective-permute-start(bf16[2,1,2,16,256]{4,3,1,0,2:T(8,128)(2,1)} %get-tuple-element.25), channel_id=1, source_target_pairs={{0,14},{1,15},{2,0},{3,1},{4,2},{5,3},{6,4},{7,5},{8,6},{9,7},{10,... | collective-permute-start | bytes 98312 | tf_op jit(solution)/shard_map/ppermute | solution.py:140
  14.3 25.6 %collective-permute-start.2 = (bf16[2,1,2,16,256]{4,3,1,0,2:T(8,128)(2,1)}, bf16[2,1,2,16,256]{4,3,1,0,2:T(8,128)(2,1)}, u32[]{:S(2)}, u32[]{:S(2)}) collective-permute-start(bf16[2,1,2,16,256]{4,3,1,0,2:T(8,128)(2,1)} %get-tuple-element.24), channel_id=1, source_target_pairs={{0,13},{1,14},{2,15},{3,0},{4,1},{5,2},{6,3},{7,4},{8,5},{9,6},{10... | collective-permute-start | bytes 98312 | tf_op jit(solution)/shard_map/ppermute | solution.py:140
  14.5 27.7 %collective-permute-start.3 = (bf16[2,1,2,16,256]{4,3,1,0,2:T(8,128)(2,1)}, bf16[2,1,2,16,256]{4,3,1,0,2:T(8,128)(2,1)}, u32[]{:S(2)}, u32[]{:S(2)}) collective-permute-start(bf16[2,1,2,16,256]{4,3,1,0,2:T(8,128)(2,1)} %get-tuple-element.23), channel_id=1, source_target_pairs={{0,12},{1,13},{2,14},{3,15},{4,0},{5,1},{6,2},{7,3},{8,4},{9,5},{1... | collective-permute-start | bytes 98312 | tf_op jit(solution)/shard_map/ppermute | solution.py:140
  15.0 29.2 %collective-permute-start.4 = (bf16[2,1,2,16,256]{4,3,1,0,2:T(8,128)(2,1)}, bf16[2,1,2,16,256]{4,3,1,0,2:T(8,128)(2,1)}, u32[]{:S(2)}, u32[]{:S(2)}) collective-permute-start(bf16[2,1,2,16,256]{4,3,1,0,2:T(8,128)(2,1)} %get-tuple-element.22), channel_id=1, source_target_pairs={{0,11},{1,12},{2,13},{3,14},{4,15},{5,0},{6,1},{7,2},{8,3},{9,4},{... | collective-permute-start | bytes 98312 | tf_op jit(solution)/shard_map/ppermute | solution.py:140
  34.0 13.6 %collective-permute-start.5 = (bf16[2,1,2,16,256]{4,3,1,0,2:T(8,128)(2,1)}, bf16[2,1,2,16,256]{4,3,1,0,2:T(8,128)(2,1)S(1)}, u32[]{:S(2)}, u32[]{:S(2)}) collective-permute-start(bf16[2,1,2,16,256]{4,3,1,0,2:T(8,128)(2,1)} %get-tuple-element.21), channel_id=1, source_target_pairs={{0,10},{1,11},{2,12},{3,13},{4,14},{5,15},{6,0},{7,1},{8,2},{9,3},... | collective-permute-start | bytes 98312 | tf_op jit(solution)/shard_map/ppermute | solution.py:140
  39.2 8.9 %collective-permute-start.6 = (bf16[2,1,2,16,256]{4,3,1,0,2:T(8,128)(2,1)}, bf16[2,1,2,16,256]{4,3,1,0,2:T(8,128)(2,1)S(1)}, u32[]{:S(2)}, u32[]{:S(2)}) collective-permute-start(bf16[2,1,2,16,256]{4,3,1,0,2:T(8,128)(2,1)} %get-tuple-element.20), channel_id=1, source_target_pairs={{0,9},{1,10},{2,11},{3,12},{4,13},{5,14},{6,15},{7,0},{8,1},{9,2},... | collective-permute-start | bytes 98312 | tf_op jit(solution)/shard_map/ppermute | solution.py:140
  39.9 10.2 %collective-permute-start.7 = (bf16[2,1,2,16,256]{4,3,1,0,2:T(8,128)(2,1)}, bf16[2,1,2,16,256]{4,3,1,0,2:T(8,128)(2,1)S(1)}, u32[]{:S(2)}, u32[]{:S(2)}) collective-permute-start(bf16[2,1,2,16,256]{4,3,1,0,2:T(8,128)(2,1)} %get-tuple-element.19), channel_id=1, source_target_pairs={{0,8},{1,9},{2,10},{3,11},{4,12},{5,13},{6,14},{7,15},{8,0},{9,1},... | collective-permute-start | bytes 98312 | tf_op jit(solution)/shard_map/ppermute | solution.py:140
  42.3 9.9 %collective-permute-start.8 = (bf16[2,1,2,16,256]{4,3,1,0,2:T(8,128)(2,1)}, bf16[2,1,2,16,256]{4,3,1,0,2:T(8,128)(2,1)S(1)}, u32[]{:S(2)}, u32[]{:S(2)}) collective-permute-start(bf16[2,1,2,16,256]{4,3,1,0,2:T(8,128)(2,1)} %get-tuple-element.18), channel_id=1, source_target_pairs={{0,7},{1,8},{2,9},{3,10},{4,11},{5,12},{6,13},{7,14},{8,15},{9,0},... | collective-permute-start | bytes 98312 | tf_op jit(solution)/shard_map/ppermute | solution.py:140
  44.2 8.6 %collective-permute-start.9 = (bf16[2,1,2,16,256]{4,3,1,0,2:T(8,128)(2,1)}, bf16[2,1,2,16,256]{4,3,1,0,2:T(8,128)(2,1)S(1)}, u32[]{:S(2)}, u32[]{:S(2)}) collective-permute-start(bf16[2,1,2,16,256]{4,3,1,0,2:T(8,128)(2,1)} %get-tuple-element.17), channel_id=1, source_target_pairs={{0,6},{1,7},{2,8},{3,9},{4,10},{5,11},{6,12},{7,13},{8,14},{9,15},... | collective-permute-start | bytes 98312 | tf_op jit(solution)/shard_map/ppermute | solution.py:140
  47.6 5.7 %collective-permute-start.10 = (bf16[2,1,2,16,256]{4,3,1,0,2:T(8,128)(2,1)}, bf16[2,1,2,16,256]{4,3,1,0,2:T(8,128)(2,1)S(1)}, u32[]{:S(2)}, u32[]{:S(2)}) collective-permute-start(bf16[2,1,2,16,256]{4,3,1,0,2:T(8,128)(2,1)} %get-tuple-element.16), channel_id=1, source_target_pairs={{0,5},{1,6},{2,7},{3,8},{4,9},{5,10},{6,11},{7,12},{8,13},{9,14},{... | collective-permute-start | bytes 98312 | tf_op jit(solution)/shard_map/ppermute | solution.py:140
  48.0 6.1 %collective-permute-start.11 = (bf16[2,1,2,16,256]{4,3,1,0,2:T(8,128)(2,1)}, bf16[2,1,2,16,256]{4,3,1,0,2:T(8,128)(2,1)S(1)}, u32[]{:S(2)}, u32[]{:S(2)}) collective-permute-start(bf16[2,1,2,16,256]{4,3,1,0,2:T(8,128)(2,1)} %get-tuple-element.15), channel_id=1, source_target_pairs={{0,4},{1,5},{2,6},{3,7},{4,8},{5,9},{6,10},{7,11},{8,12},{9,13},{1... | collective-permute-start | bytes 98312 | tf_op jit(solution)/shard_map/ppermute | solution.py:140
  50.1 6.2 %collective-permute-start.12 = (bf16[2,1,2,16,256]{4,3,1,0,2:T(8,128)(2,1)}, bf16[2,1,2,16,256]{4,3,1,0,2:T(8,128)(2,1)S(1)}, u32[]{:S(2)}, u32[]{:S(2)}) collective-permute-start(bf16[2,1,2,16,256]{4,3,1,0,2:T(8,128)(2,1)} %get-tuple-element.14), channel_id=1, source_target_pairs={{0,3},{1,4},{2,5},{3,6},{4,7},{5,8},{6,9},{7,10},{8,11},{9,12},{10... | collective-permute-start | bytes 98312 | tf_op jit(solution)/shard_map/ppermute | solution.py:140
  52.2 7.2 %collective-permute-start.13 = (bf16[2,1,2,16,256]{4,3,1,0,2:T(8,128)(2,1)}, bf16[2,1,2,16,256]{4,3,1,0,2:T(8,128)(2,1)S(1)}, u32[]{:S(2)}, u32[]{:S(2)}) collective-permute-start(bf16[2,1,2,16,256]{4,3,1,0,2:T(8,128)(2,1)} %get-tuple-element.13), channel_id=1, source_target_pairs={{0,2},{1,3},{2,4},{3,5},{4,6},{5,7},{6,8},{7,9},{8,10},{9,11},{10,... | collective-permute-start | bytes 98312 | tf_op jit(solution)/shard_map/ppermute | solution.py:140
  52.7 6.6 %collective-permute-start.14 = (bf16[2,1,2,16,256]{4,3,1,0,2:T(8,128)(2,1)}, bf16[2,1,2,16,256]{4,3,1,0,2:T(8,128)(2,1)S(1)}, u32[]{:S(2)}, u32[]{:S(2)}) collective-permute-start(bf16[2,1,2,16,256]{4,3,1,0,2:T(8,128)(2,1)} %get-tuple-element.12), channel_id=1, source_target_pairs={{0,1},{1,2},{2,3},{3,4},{4,5},{5,6},{6,7},{7,8},{8,9},{9,10},{10,1... | collective-permute-start | bytes 98312 | tf_op jit(solution)/shard_map/ppermute | solution.py:140
  70.8 5.2 %collective-permute-start.15 = (bf16[8,4224]{1,0:T(8,128)(2,1)S(1)}, bf16[8,4224]{1,0:T(8,128)(2,1)S(1)}, u32[]{:S(2)}, u32[]{:S(2)}) collective-permute-start(bf16[8,4224]{1,0:T(8,128)(2,1)S(1)} %get-tuple-element.27), channel_id=1, source_target_pairs={{0,8},{1,9},{2,10},{3,11},{4,12},{5,13},{6,14},{7,15},{8,0},{9,1},... | collective-permute-start | bytes 202760 | tf_op jit(solution)/shard_map/ppermute | solution.py:20
  76.0 5.1 %collective-permute-start.16 = (bf16[16,4224]{1,0:T(8,128)(2,1)S(1)}, bf16[16,4224]{1,0:T(8,128)(2,1)S(1)}, u32[]{:S(2)}, u32[]{:S(2)}) collective-permute-start(bf16[16,4224]{1,0:T(8,128)(2,1)S(1)} %pad_maximum_fusion.2), channel_id=1, source_target_pairs={{0,4},{1,5},{2,6},{3,7},{4,0},{5,1},{6,2},{7,3},{8,12},{9,13},{10,... | collective-permute-start | bytes 405512 | tf_op jit(solution)/shard_map/ppermute | solution.py:20
  81.1 6.5 %collective-permute-start.17 = (bf16[32,4224]{1,0:T(8,128)(2,1)S(1)}, bf16[32,4224]{1,0:T(8,128)(2,1)S(1)}, u32[]{:S(2)}, u32[]{:S(2)}) collective-permute-start(bf16[32,4224]{1,0:T(8,128)(2,1)S(1)} %pad_maximum_fusion.1), channel_id=1, source_target_pairs={{0,2},{1,3},{2,0},{3,1},{4,6},{5,7},{6,4},{7,5},{8,10},{9,11},{10,... | collective-permute-start | bytes 811016 | tf_op jit(solution)/shard_map/ppermute | solution.py:20
  87.7 2.0 %collective-permute-start.18 = (bf16[64,4224]{1,0:T(8,128)(2,1)S(1)}, bf16[64,4224]{1,0:T(8,128)(2,1)S(1)}, u32[]{:S(2)}, u32[]{:S(2)}) collective-permute-start(bf16[64,4224]{1,0:T(8,128)(2,1)S(1)} %pad_maximum_fusion), channel_id=1, source_target_pairs={{0,1},{1,0},{2,3},{3,2},{4,5},{5,4},{6,7},{7,6},{8,9},{9,8},{10,11... | collective-permute-start | bytes 1622024 | tf_op jit(solution)/shard_map/ppermute | solution.py:20
  99.6 2.0 %collective-permute-start.19 = (bf16[64,4096]{1,0:T(8,128)(2,1)S(1)}, bf16[64,4096]{1,0:T(8,128)(2,1)S(1)}, u32[]{:S(2)}, u32[]{:S(2)}) collective-permute-start(bf16[64,4096]{1,0:T(8,128)(2,1)S(1)} %slice.227), channel_id=1, source_target_pairs={{0,1},{1,0},{2,3},{3,2},{4,5},{5,4},{6,7},{7,6},{8,9},{9,8},{10,11... | collective-permute-start | bytes 1572872 | tf_op jit(solution)/shard_map/ppermute | solution.py:20
  103.0 8.4 %collective-permute-start.20 = (bf16[32,4096]{1,0:T(8,128)(2,1)S(1)}, bf16[32,4096]{1,0:T(8,128)(2,1)S(1)}, u32[]{:S(2)}, u32[]{:S(2)}) collective-permute-start(bf16[32,4096]{1,0:T(8,128)(2,1)S(1)} %slice.228), channel_id=1, source_target_pairs={{0,2},{1,3},{2,0},{3,1},{4,6},{5,7},{6,4},{7,5},{8,10},{9,11},{10,... | collective-permute-start | bytes 786440 | tf_op jit(solution)/shard_map/ppermute | solution.py:20
  111.5 5.0 %collective-permute-start.21 = (bf16[16,4096]{1,0:T(8,128)(2,1)S(1)}, bf16[16,4096]{1,0:T(8,128)(2,1)S(1)}, u32[]{:S(2)}, u32[]{:S(2)}) collective-permute-start(bf16[16,4096]{1,0:T(8,128)(2,1)S(1)} %slice.229), channel_id=1, source_target_pairs={{0,4},{1,5},{2,6},{3,7},{4,0},{5,1},{6,2},{7,3},{8,12},{9,13},{10,... | collective-permute-start | bytes 393224 | tf_op jit(solution)/shard_map/ppermute | solution.py:20
  116.5 5.4 %collective-permute-start.22 = (bf16[8,4096]{1,0:T(8,128)(2,1)S(1)}, bf16[8,4096]{1,0:T(8,128)(2,1)S(1)}, u32[]{:S(2)}, u32[]{:S(2)}) collective-permute-start(bf16[8,4096]{1,0:T(8,128)(2,1)S(1)} %slice.230), channel_id=1, source_target_pairs={{0,8},{1,9},{2,10},{3,11},{4,12},{5,13},{6,14},{7,15},{8,0},{9,1},... | collective-permute-start | bytes 196616 | tf_op jit(solution)/shard_map/ppermute | solution.py:20
  (14 other events, 92.2 us)
